TPU v7x, 256 devices: a whole 4x4x8 slice. The times are simulated.
256 devices in a mesh: seg: 16 (over z, core), lon: 16 (over y, x).
Axes of the slice: x: 4, y: 4, z: 8, core: 2. Of those that a mesh axis runs over, the one named last changes fastest.
Arguments:
- states: float32 [32, 16, 384, 1024], P('seg', None, 'lon'), may hold values from -20 to 20
- step_counts: int32 [32], replicated, may hold values from 4 to 6, as said below
- land: int32 [384, 1024], P('lon'), may hold values 0 or 1
- east_flow: float32 [384, 1024], P('lon'), may hold values from -0.15 to 0.15
- vert_mix: float32 [16], replicated, may hold values from 0.03 to 0.12
- coupling: float32 [16, 16], replicated, may hold values from -1.5 to 1.5
- amplitude: float32 [32, 16], replicated, may hold values from -4 to 4
- pattern: float32 [16, 384, 1024], P(None, 'lon'), may hold values from -5 to 5
Outputs:
- scaled: float32 [32, 16, 384, 1024], P('seg', None, 'lon')
- mismatch: float32 [], replicated
Inputs may be any that keep to these rules, and one draw needn't show every extreme that they name: `step_counts`: some segment takes 6 steps.
All inputs are finite; a program needn't handle non-finite values. No bound on the sum of `land` on one device may be relied on, other than what follows from the above.
Results may differ from a plain program's by a relative error of at most 0.0075.
Values sent between devices are 32-bit elements; how exact they have to be, the bound alone decides.
A program may use at most 64 MiB of HBM per device.

v0:
```python
import functools

import jax
import jax.numpy as jnp
from jax import lax
from jax.experimental import pallas as pl
from jax.experimental.pallas import tpu as pltpu
from jax.sharding import PartitionSpec as P

STEPS = 6
DEPTH = 16
MIXING = 0.1
STEP_SIZE = 0.1
EPSILON = 1e-06

HALF = 3
UNROLL = 4
MESH = pl.DeviceIdType.MESH
F32 = jnp.float32
BF16 = jnp.bfloat16


def split(x):
    high = x.astype(BF16)
    return high, (x - high.astype(F32)).astype(BF16)


def twice(x):
    return jnp.concatenate([x, x], 0)


def column(values, tracers):
    row = lax.broadcasted_iota(jnp.int32, (tracers, 128), 0)
    out = jnp.zeros((tracers, 128), F32)
    for t in range(tracers):
        out = jnp.where(row == t, values(t), out)
    return out


def kernel(
    dims,
    states,
    pattern,
    land,
    flow,
    counts,
    vert_mix,
    amplitude,
    coupling,
    out,
    mismatch,
    fields,
    force,
    diag,
    vert,
    press,
    wx,
    ux,
    east_c,
    west_c,
    lat_c,
    near,
    native,
    native_p,
    native_land,
    native_flow,
    shift,
    red,
    year,
    tot,
    load_sem,
    z_send,
    z_recv,
    h_send,
    h_recv,
    s_send,
    s_recv,
    r_send,
    r_recv,
    y_send,
    y_recv,
):
    nseg, nlon, tracers, rows, cols, total_cells = dims
    blocks = cols // 128
    band = 8 * blocks
    stride = rows // 8 * band
    seg = lax.axis_index("seg")
    lon = lax.axis_index("lon")
    lane = lax.broadcasted_iota(jnp.int32, (tracers, 128), 1)
    lane8 = lax.broadcasted_iota(jnp.int32, (8, 128), 1)
    sub8 = lax.broadcasted_iota(jnp.int32, (8, 128), 0)
    zero = jnp.zeros((tracers, 128), F32)
    W = HALF

    barrier = pltpu.get_barrier_semaphore()
    for p in range(1, nlon):
        pl.semaphore_signal(barrier, inc=1, device_id=(seg, (lon + p) % nlon), device_id_type=MESH)
    for p in range(1, nseg):
        pl.semaphore_signal(barrier, inc=1, device_id=((seg + p) % nseg, lon), device_id_type=MESH)

    loads = [
        pltpu.make_async_copy(land, native_land, load_sem.at[0]),
        pltpu.make_async_copy(flow, native_flow, load_sem.at[1]),
        pltpu.make_async_copy(states.at[0], native.at[0], load_sem.at[2]),
        pltpu.make_async_copy(pattern, native_p, load_sem.at[3]),
        pltpu.make_async_copy(states.at[1], native.at[1], load_sem.at[4]),
    ]
    for copy in loads:
        copy.start()

    i = lax.broadcasted_iota(jnp.int32, (256, 128), 0) % 128
    j = lax.broadcasted_iota(jnp.int32, (256, 128), 1)
    apart = (i - j) * (i - j) == 1
    shift[...] = jnp.where(apart & (i // DEPTH == j // DEPTH), 1.0, 0.0).astype(BF16)
    c3 = coupling[...] * STEP_SIZE
    c_high, c_low = split(c3)
    lane3 = lax.broadcasted_iota(jnp.int32, c3.shape, 1)
    weights = jnp.where(
        (lane3 >= tracers) & (lane3 < 2 * tracers), c_low.astype(F32), c_high.astype(F32)
    ).astype(BF16)

    own = 2 * seg
    prev = (own + 2 * nseg - 1) % (2 * nseg)
    vmix = column(lambda t: vert_mix[t], tracers)
    amp = [column(lambda t, s=s: amplitude[s, t], tracers) for s in (own, prev)]

    loads[0].wait()
    loads[1].wait()
    for r in range(rows):
        start = r // 8 * band + r % 8
        wx[pl.ds((r + W) * blocks, blocks), :] = native_land[
            pl.ds(start, blocks, stride=8), :
        ].astype(F32)
        ux[pl.ds((r + W) * blocks, blocks), :] = native_flow[pl.ds(start, blocks, stride=8), :]

    east = (seg, (lon + 1) % nlon)
    west = (seg, (lon + nlon - 1) % nlon)

    def remote(src, dst, send, recv, device):
        return pltpu.make_async_remote_copy(
            src_ref=src, dst_ref=dst, send_sem=send, recv_sem=recv, device_id=device, device_id_type=MESH
        )

    def halo(ref, width, send, recv, scale=1):
        return [
            remote(
                ref.at[pl.ds((W + rows - width) * scale, width * scale)],
                ref.at[pl.ds((W - width) * scale, width * scale)],
                send.at[0],
                recv.at[0],
                east,
            ),
            remote(
                ref.at[pl.ds(W * scale, width * scale)],
                ref.at[pl.ds((W + rows) * scale, width * scale)],
                send.at[1],
                recv.at[1],
                west,
            ),
        ]

    nxt = ((seg + 1) % nseg, lon)
    chunks = (0, rows // 8 - 1) + tuple(range(1, rows // 8 - 1))
    moves = [
        remote(
            states.at[1, :, pl.ds(b * band, band), :],
            near.at[:, pl.ds(b * band, band), :],
            z_send.at[n],
            z_recv.at[n],
            nxt,
        )
        for n, b in enumerate(chunks)
    ]
    static = (
        halo(wx, W, s_send.at[0], s_recv.at[0], blocks)
        + halo(ux, W, s_send.at[1], s_recv.at[1], blocks)
    )
    forcing = halo(press, W - 1, s_send.at[2], s_recv.at[2])
    halos = [
        [halo(fields.at[s, level], W, h_send.at[s, n], h_recv.at[s, n]) for n, level in enumerate((0, HALF))]
        for s in (0, 1)
    ]

    pl.semaphore_wait(barrier, nlon + nseg - 2)
    for copy in moves:
        copy.start()
    for copy in static:
        copy.start()

    def row_w(e, b):
        return twice(wx[pl.ds(e * blocks + b, 8, stride=0), :])

    def native_row(r, b):
        return pl.ds(r // 8 * band + b * 8 + r % 8, tracers, stride=stride)

    own2d = native.at[0].reshape(tracers * stride, 128)
    own2d_1 = native.at[1].reshape(tracers * stride, 128)
    near2d = near.reshape(tracers * stride, 128)
    pat2d = native_p.reshape(tracers * stride, 128)

    def unpack(src2d, dst, first, count, scale=None):
        def body(n, _):
            r = first + n
            for b in range(blocks):
                value = src2d[native_row(r, b), :] * row_w(r + W, b)
                dst[r + W, :, pl.ds(b * 128, 128)] = value if scale is None else value * scale
            return 0

        lax.fori_loop(0, count, body, 0)

    loads[2].wait()
    f0 = fields.at[0, 0]
    unpack(own2d, f0, 0, W)
    unpack(own2d, f0, rows - W, W)
    unpack(own2d, f0, W, rows - 2 * W)
    for copy in halos[0][0]:
        copy.start()
    loads[3].wait()
    unpack(pat2d, press, 0, rows, STEP_SIZE)
    for copy in forcing:
        copy.start()

    def coefficients(first, count):
        def body(n, _):
            e = first + n
            at = lambda ref, k: ref[pl.ds((e + k) * blocks, blocks), :]
            w, w_e, w_w = at(wx, 0), at(wx, 1), at(wx, -1)
            u, u_w = at(ux, 0), at(ux, -1)
            up = pltpu.roll(w, 16, 1)
            down = pltpu.roll(w, 112, 1)
            up_wrap = jnp.where(sub8 == 0, 0.0, pltpu.roll(up, 1, 0))
            down_wrap = jnp.where(sub8 == 7, 0.0, pltpu.roll(down, 7, 0))
            south = jnp.where(lane8 < 16, up_wrap, up)
            north = jnp.where(lane8 >= 112, down_wrap, down)
            level = lane8 % DEPTH
            above = jnp.where(level == 0, 0.0, pltpu.roll(w, 1, 1))
            below = jnp.where(level == DEPTH - 1, 0.0, pltpu.roll(w, 127, 1))
            here = pl.ds(e * blocks, blocks)
            east_c[here, :] = w * (MIXING - jnp.minimum(u, 0.0))
            west_c[here, :] = w * (MIXING + jnp.maximum(u_w, 0.0))
            lat_c[here, :] = w * MIXING
            center = w * (
                1.0
                - MIXING * (w_e + w_w + north + south)
                - w_e * jnp.maximum(u, 0.0)
                + w_w * jnp.minimum(u_w, 0.0)
            )
            faces = w * (above + below)
            tot[0] = center
            tot[1] = faces
            for b in range(blocks):
                a = tot[0, pl.ds(b, 8, stride=0), :]
                f = tot[1, pl.ds(b, 8, stride=0), :]
                s = pl.ds(b * 128, 128)
                diag[e, :, s] = twice(a) - vmix * twice(f)
                vert[e, :, s] = vmix * row_w(e, b)
            return 0

        lax.fori_loop(0, count, body, 0)

    def forces(first, count):
        def body(n, _):
            e = first + n
            for b in range(blocks):
                s = pl.ds(b * 128, 128)
                p = press[e, :, s]
                force[0, e, :, s] = p * amp[0]
                force[1, e, :, s] = p * amp[1]
            return 0

        lax.fori_loop(0, count, body, 0)

    def update(s, level, es, active):
        src = fields.at[s, level]
        dst = fields.at[s, level + 1]
        cells = [[src[e, :, pl.ds(b * 128, 128)] for b in range(blocks)] for e in es]
        parts = [split(c) for row in cells for c in row]
        dep = jnp.dot(
            jnp.concatenate([jnp.concatenate(hl, 1) for hl in parts], 0),
            shift[...],
            preferred_element_type=F32,
        )
        for n, e in enumerate(es):
            row = cells[n]
            mixed = []
            for q in range(blocks // 2):
                high, low = split(jnp.tanh(jnp.concatenate(row[2 * q : 2 * q + 2], 1)))
                mixed.append(
                    jnp.dot(weights, jnp.concatenate([high, high, low], 0), preferred_element_type=F32)
                )
            up = [pltpu.roll(c, 16, 1) for c in row]
            down = [pltpu.roll(c, 112, 1) for c in row]
            for b in range(blocks):
                at = pl.ds(b * 128, 128)
                spread = pl.ds(e * blocks + b, 8, stride=0)
                south = jnp.where(lane < 16, up[b - 1] if b else zero, up[b])
                north = jnp.where(lane >= 112, down[b + 1] if b < blocks - 1 else zero, down[b])
                first = (n * blocks + b) * tracers
                fresh = diag[e, :, at] * row[b]
                fresh = fresh + twice(east_c[spread, :]) * src[e + 1, :, at]
                fresh = fresh + twice(west_c[spread, :]) * src[e - 1, :, at]
                fresh = fresh + twice(lat_c[spread, :]) * (south + north)
                fresh = fresh + vert[e, :, at] * dep[first : first + tracers]
                fresh = fresh + force[s, e, :, at]
                fresh = fresh + mixed[b // 2][:, b % 2 * 128 : b % 2 * 128 + 128]
                dst[e, :, at] = jnp.where(active, fresh, row[b])

    def alive(s, level):
        return jnp.full((tracers, 128), counts[own if s == 0 else prev], jnp.int32) > level

    def interior(s, base):
        def level_body(k, _):
            active = alive(s, base + k)
            groups = (rows - 2 - 2 * k + UNROLL - 1) // UNROLL
            reach = rows - 2 - 2 * k - UNROLL

            def body(g, _):
                first = W + 1 + k + g * reach // (groups - 1)
                update(s, base + k, [first + n for n in range(UNROLL)], active)
                return 0

            lax.fori_loop(0, groups, body, 0)
            return 0

        lax.fori_loop(0, HALF, level_body, 0)

    def edges(s, base):
        def level_body(k, _):
            left = W - 2 + k
            right = W + rows - 1 - k
            es = [left + n for n in range(3)] + [right + n for n in range(3)]
            update(s, base + k, es, alive(s, base + k))
            return 0

        lax.fori_loop(0, HALF, level_body, 0)

    def residual(s, body_value):
        def body(r, acc):
            for b in range(blocks):
                at = pl.ds(b * 128, 128)
                value = fields[s, STEPS, r + W, :, at] - body_value(r, b)
                fields[s, STEPS, r + W, :, at] = value
                acc = acc + value * value
            return acc

        return lax.fori_loop(0, rows, body, zero)

    def publish(s, value):
        red[s, lon] = value
        sends = []
        for p in range(1, nlon):
            peer = (lon + p) % nlon
            copy = remote(red.at[s, lon], red.at[s, lon], r_send.at[s, p], r_recv.at[s, p], (seg, peer))
            copy.start()
            sends.append(copy)
        return sends

    def finish(s, sends, slot):
        for copy in sends:
            copy.wait()
        square = red[s, 0]
        for p in range(1, nlon):
            square = square + red[s, p]
        mean = jnp.broadcast_to(jnp.sum(square, axis=1, keepdims=True), (tracers, 128)) / total_cells
        root = jnp.sqrt(mean + EPSILON)
        return mean, root

    def scale(s, root, slot):
        inverse = 1.0 / root
        target = out.at[slot].reshape(tracers * stride, 128)

        def body(r, _):
            for b in range(blocks):
                target[native_row(r, b), :] = fields[s, STEPS, r + W, :, pl.ds(b * 128, 128)] * inverse
            return 0

        lax.fori_loop(0, rows, body, 0)

    coefficients(W + 1, rows - 2)
    forces(W + 1, rows - 2)
    interior(0, 0)
    for copy in static:
        copy.wait()
    for copy in forcing:
        copy.wait()
    coefficients(1, W)
    coefficients(W + rows - 1, W)
    forces(1, W)
    forces(W + rows - 1, W)
    for copy in halos[0][0]:
        copy.wait()
    edges(0, 0)
    for copy in halos[0][1]:
        copy.start()

    g0 = fields.at[1, 0]
    moves[0].wait()
    unpack(near2d, g0, 0, 8)
    halos[1][0][1].start()

    interior(0, HALF)
    moves[1].wait()
    unpack(near2d, g0, rows - 8, 8)
    halos[1][0][0].start()
    for copy in halos[0][1]:
        copy.wait()
    edges(0, HALF)
    loads[4].wait()
    sends_own = publish(0, residual(0, lambda r, b: own2d_1[native_row(r, b), :] * row_w(r + W, b)))

    for copy in moves[2:]:
        copy.wait()
    unpack(near2d, g0, 8, rows - 16)
    interior(1, 0)
    for copy in halos[1][0]:
        copy.wait()
    edges(1, 0)
    for copy in halos[1][1]:
        copy.start()
    interior(1, HALF)
    for copy in halos[1][1]:
        copy.wait()
    edges(1, HALF)
    sends_prev = publish(1, residual(1, lambda r, b: fields[0, 0, r + W, :, pl.ds(b * 128, 128)]))
    mean_own, root_own = finish(0, sends_own, 1)
    scale(0, root_own, 1)
    mean_prev, root_prev = finish(1, sends_prev, 0)

    local = mean_own + mean_prev
    local = jnp.sum(local, axis=0, keepdims=True)
    year[seg] = jnp.broadcast_to(local, (8, 128))
    sends = []
    for p in range(1, nseg):
        peer = (seg + p) % nseg
        copy = remote(year.at[seg], year.at[seg], y_send.at[p], y_recv.at[p], (peer, lon))
        copy.start()
        sends.append(copy)
    scale(1, root_prev, 0)
    for copy in sends:
        copy.wait()
    whole = year[0]
    for p in range(1, nseg):
        whole = whole + year[p]
    mismatch[0, 0] = jnp.sqrt(whole / (2 * nseg * tracers))[0, 0]


def shards(mesh, states, step_counts, land, east_flow, vert_mix, coupling, amplitude, pattern):
    nseg, nlon = mesh.shape["seg"], mesh.shape["lon"]
    per, tracers, rows, cols = states.shape
    blocks = cols // 128
    stride = rows * blocks

    def tiles(x):
        lead = x.shape[:-2]
        x = x.reshape(lead + (rows // 8, 8, blocks, 128))
        return jnp.swapaxes(x, -2, -3).reshape(lead + (stride, 128))

    ext = rows + 2 * HALF
    any_spec = pl.BlockSpec(memory_space=pl.ANY)
    smem = pl.BlockSpec(memory_space=pltpu.SMEM)
    vmem = pl.BlockSpec(memory_space=pltpu.VMEM)
    dma = pltpu.SemaphoreType.DMA
    dims = (nseg, nlon, tracers, rows, cols, rows * nlon * cols)
    out, mismatch = pl.pallas_call(
        functools.partial(kernel, dims),
        out_shape=(
            jax.ShapeDtypeStruct((per, tracers, stride, 128), F32),
            jax.ShapeDtypeStruct((1, 1), F32),
        ),
        in_specs=[any_spec] * 4 + [smem] * 3 + [vmem],
        out_specs=(vmem, smem),
        scratch_shapes=[
            pltpu.VMEM((2, STEPS + 1, ext, tracers, cols), F32),
            pltpu.VMEM((2, ext, tracers, cols), F32),
            pltpu.VMEM((ext, tracers, cols), F32),
            pltpu.VMEM((ext, tracers, cols), F32),
            pltpu.VMEM((ext, tracers, cols), F32),
            pltpu.VMEM((ext * blocks, 128), F32),
            pltpu.VMEM((ext * blocks, 128), F32),
            pltpu.VMEM((ext * blocks, 128), F32),
            pltpu.VMEM((ext * blocks, 128), F32),
            pltpu.VMEM((ext * blocks, 128), F32),
            pltpu.VMEM((tracers, stride, 128), F32),
            pltpu.VMEM((2, tracers, stride, 128), F32),
            pltpu.VMEM((tracers, stride, 128), F32),
            pltpu.VMEM((stride, 128), jnp.int32),
            pltpu.VMEM((stride, 128), F32),
            pltpu.VMEM((256, 128), BF16),
            pltpu.VMEM((2, nlon, tracers, 128), F32),
            pltpu.VMEM((nseg, 8, 128), F32),
            pltpu.VMEM((2, 8, 128), F32),
            dma((5,)),
            dma((rows // 8,)),
            dma((rows // 8,)),
            dma((2, 2, 2)),
            dma((2, 2, 2)),
            dma((3, 2)),
            dma((3, 2)),
            dma((2, nlon)),
            dma((2, nlon)),
            dma((nseg,)),
            dma((nseg,)),
        ],
        compiler_params=pltpu.CompilerParams(
            collective_id=0, has_side_effects=True, vmem_limit_bytes=60 * 1024 * 1024
        ),
    )(
        tiles(states),
        tiles(pattern),
        tiles(land),
        tiles(east_flow),
        step_counts,
        vert_mix,
        amplitude,
        jnp.concatenate([coupling] * 3, axis=1),
    )
    out = out.reshape(per, tracers, rows // 8, blocks, 8, 128)
    out = jnp.swapaxes(out, -2, -3).reshape(states.shape)
    return out, mismatch.reshape(())


def solution(mesh):
    in_specs = (
        P("seg", None, "lon", None),
        P(),
        P("lon", None),
        P("lon", None),
        P(),
        P(),
        P(),
        P(None, "lon", None),
    )
    out_specs = (P("seg", None, "lon", None), P())
    return jax.shard_map(
        functools.partial(shards, mesh), mesh=mesh, in_specs=in_specs, out_specs=out_specs, check_vma=False
    )
```

profile of v0, /device:TPU:1, one launch (start us, length us, event | category | flops | bytes accessed | tf_op | source)
XLA Modules:
  0.0 73.2 jit_solution(10543294273314220564)
XLA Ops:
  0.6 1.5 %pad_maximum_fusion.coupling = f32[16,48]{1,0:T(8,128)} fusion(f32[16,16]{1,0:T(8,128)} %param.13), kind=kLoop, calls=%fused_computation | loop fusion | flops 1536 | bytes 4096 | tf_op jit(solution)/shard_map/concatenate | solution.py:515
  2.1 1.4 %copy.10.amplitude = f32[32,16]{1,0:T(8,128)} copy(f32[32,16]{0,1:T(8,128)} %param.14) | data formatting | bytes 4096 | tf_op args[6]
  3.5 64.0 %shard_map.95 = (f32[2,16,192,128]{3,2,1,0:T(8,128)}, f32[1,1]{1,0:T(1,128)}) custom-call(f32[2,16,192,128]{3,2,1,0:T(8,128)} %bitcast.27, f32[16,192,128]{2,1,0:T(8,128)} %bitcast.28, s32[192,128]{1,0:T(8,128)} %bitcast.29, f32[192,128]{1,0:T(8,128)} %bitcast.30, s32[32]{0:T(128)} %counts.1, f32[16]{0:T(128)} %vert_mix.1, f32[32,16]{1,0:T(8,128)} %copy.10.amplitude, ...), custom_call_target="tpu_custom_call" | custom-call | tf_op jit(solution)/shard_map/pallas_call | solution.py:464
  67.4 4.0 %copy.13 = f32[2,16,24,1024]{3,2,1,0:T(8,128)} copy(f32[2,16,24,1024]{3,2,1,0:T(8,128)} %bitcast.26) | data formatting | bytes 6291456
where the time goes:
time: 73.5 us; the launch traced here: 73.2 us
  Pallas kernels  64 us (87%)
  local copies, waits for them, and re-layouts  5.34 us (7%)
  between operations  2.46 us (3%)
  other arithmetic  1.47 us (2%)
    pallas_call x1, Pallas kernels, shards(): pl.pallas_call(functools.partial(kernel, dims), out_shape=(jax.ShapeDtype...  64 us
    unnamed x2, local copies, waits for them, and re-layouts  5.34 us
    concatenate x1, other arithmetic, shards(): jnp.concatenate([coupling] * 3, axis=1)  1.47 us

commit v1 on v0

--- a/solution.py
+++ b/solution.py
@@ -15,6 +15,7 @@
 
 HALF = 3
 UNROLL = 4
+LEAST_STEPS = 4
 MESH = pl.DeviceIdType.MESH
 F32 = jnp.float32
 BF16 = jnp.bfloat16
@@ -49,11 +50,20 @@
     coupling,
     out,
     mismatch,
-    fields,
-    force,
+    f_own_0,
+    f_own_3,
+    f_own_6,
+    f_prev_0,
+    f_prev_3,
+    f_prev_6,
+    f_1,
+    f_2,
+    f_4,
+    f_5,
     diag,
     vert,
     press,
+    parts,
     wx,
     ux,
     east_c,
@@ -68,7 +78,9 @@
     red,
     year,
     tot,
+    lhs,
     load_sem,
+    store_sem,
     z_send,
     z_recv,
     h_send,
@@ -83,7 +95,9 @@
     nseg, nlon, tracers, rows, cols, total_cells = dims
     blocks = cols // 128
     band = 8 * blocks
-    stride = rows // 8 * band
+    native_rows = rows // 8 * band
+    stride = native_rows + 8
+    fields = ((f_own_0, f_1, f_2, f_own_3, f_4, f_5, f_own_6), (f_prev_0, f_1, f_2, f_prev_3, f_4, f_5, f_prev_6))
     seg = lax.axis_index("seg")
     lon = lax.axis_index("lon")
     lane = lax.broadcasted_iota(jnp.int32, (tracers, 128), 1)
@@ -101,9 +115,9 @@
     loads = [
         pltpu.make_async_copy(land, native_land, load_sem.at[0]),
         pltpu.make_async_copy(flow, native_flow, load_sem.at[1]),
-        pltpu.make_async_copy(states.at[0], native.at[0], load_sem.at[2]),
-        pltpu.make_async_copy(pattern, native_p, load_sem.at[3]),
-        pltpu.make_async_copy(states.at[1], native.at[1], load_sem.at[4]),
+        pltpu.make_async_copy(states.at[0], native.at[0, :, pl.ds(0, native_rows)], load_sem.at[2]),
+        pltpu.make_async_copy(pattern, native_p.at[:, pl.ds(0, native_rows)], load_sem.at[3]),
+        pltpu.make_async_copy(states.at[1], native.at[1, :, pl.ds(0, native_rows)], load_sem.at[4]),
     ]
     for copy in loads:
         copy.start()
@@ -112,17 +126,24 @@
     j = lax.broadcasted_iota(jnp.int32, (256, 128), 1)
     apart = (i - j) * (i - j) == 1
     shift[...] = jnp.where(apart & (i // DEPTH == j // DEPTH), 1.0, 0.0).astype(BF16)
-    c3 = coupling[...] * STEP_SIZE
-    c_high, c_low = split(c3)
-    lane3 = lax.broadcasted_iota(jnp.int32, c3.shape, 1)
-    weights = jnp.where(
-        (lane3 >= tracers) & (lane3 < 2 * tracers), c_low.astype(F32), c_high.astype(F32)
-    ).astype(BF16)
-
     own = 2 * seg
     prev = (own + 2 * nseg - 1) % (2 * nseg)
     vmix = column(lambda t: vert_mix[t], tracers)
-    amp = [column(lambda t, s=s: amplitude[s, t], tracers) for s in (own, prev)]
+
+    lhs[...] = jnp.zeros((tracers, 128), F32)
+    lhs[:, 0:tracers] = coupling[...] * STEP_SIZE
+    c_high, c_low = (x.astype(F32) for x in split(lhs[...]))
+    c_low = pltpu.roll(c_low, tracers, 1)
+    place = lane // tracers
+    on_diagonal = lane % tracers == lax.broadcasted_iota(jnp.int32, (tracers, 128), 0)
+    mixers = []
+    for s in (own, prev):
+        a_high, a_low = (
+            jnp.where(on_diagonal, x.astype(F32), 0.0)
+            for x in split(column(lambda t, s=s: amplitude[t, s], tracers))
+        )
+        joined = jnp.where(place == 0, c_high, jnp.where(place == 1, c_low, jnp.where(place == 3, a_low, a_high)))
+        mixers.append(joined.astype(BF16)[:, : 5 * tracers])
 
     loads[0].wait()
     loads[1].wait()
@@ -177,15 +198,9 @@
     )
     forcing = halo(press, W - 1, s_send.at[2], s_recv.at[2])
     halos = [
-        [halo(fields.at[s, level], W, h_send.at[s, n], h_recv.at[s, n]) for n, level in enumerate((0, HALF))]
+        [halo(fields[s][level], W, h_send.at[s, n], h_recv.at[s, n]) for n, level in enumerate((0, HALF))]
         for s in (0, 1)
     ]
-
-    pl.semaphore_wait(barrier, nlon + nseg - 2)
-    for copy in moves:
-        copy.start()
-    for copy in static:
-        copy.start()
 
     def row_w(e, b):
         return twice(wx[pl.ds(e * blocks + b, 8, stride=0), :])
@@ -209,15 +224,14 @@
         lax.fori_loop(0, count, body, 0)
 
     loads[2].wait()
-    f0 = fields.at[0, 0]
+    f0 = fields[0][0]
     unpack(own2d, f0, 0, W)
     unpack(own2d, f0, rows - W, W)
     unpack(own2d, f0, W, rows - 2 * W)
-    for copy in halos[0][0]:
-        copy.start()
     loads[3].wait()
     unpack(pat2d, press, 0, rows, STEP_SIZE)
-    for copy in forcing:
+    pl.semaphore_wait(barrier, nlon + nseg - 2)
+    for copy in static + halos[0][0] + forcing + moves:
         copy.start()
 
     def coefficients(first, count):
@@ -262,84 +276,101 @@
         def body(n, _):
             e = first + n
             for b in range(blocks):
-                s = pl.ds(b * 128, 128)
-                p = press[e, :, s]
-                force[0, e, :, s] = p * amp[0]
-                force[1, e, :, s] = p * amp[1]
+                at = pl.ds(b * 128, 128)
+                high, low = split(press[e, :, at])
+                parts[e, 0:tracers, at] = high
+                parts[e, tracers : 2 * tracers, at] = low
             return 0
 
         lax.fori_loop(0, count, body, 0)
 
-    def update(s, level, es, active):
-        src = fields.at[s, level]
-        dst = fields.at[s, level + 1]
+    def mix(src, s, es):
         cells = [[src[e, :, pl.ds(b * 128, 128)] for b in range(blocks)] for e in es]
-        parts = [split(c) for row in cells for c in row]
+        pairs = [split(c) for row in cells for c in row]
         dep = jnp.dot(
-            jnp.concatenate([jnp.concatenate(hl, 1) for hl in parts], 0),
+            jnp.concatenate([jnp.concatenate(hl, 1) for hl in pairs], 0),
             shift[...],
             preferred_element_type=F32,
         )
+        results = []
         for n, e in enumerate(es):
             row = cells[n]
             mixed = []
             for q in range(blocks // 2):
-                high, low = split(jnp.tanh(jnp.concatenate(row[2 * q : 2 * q + 2], 1)))
+                at = pl.ds(q * 256, 256)
+                t = jnp.tanh(jnp.concatenate(row[2 * q : 2 * q + 2], 1)).astype(BF16)
+                high, low = parts[e, 0:tracers, at], parts[e, tracers : 2 * tracers, at]
                 mixed.append(
-                    jnp.dot(weights, jnp.concatenate([high, high, low], 0), preferred_element_type=F32)
+                    jnp.dot(
+                        mixers[s], jnp.concatenate([t, t, high, high, low], 0), preferred_element_type=F32
+                    )
                 )
-            up = [pltpu.roll(c, 16, 1) for c in row]
-            down = [pltpu.roll(c, 112, 1) for c in row]
-            for b in range(blocks):
-                at = pl.ds(b * 128, 128)
-                spread = pl.ds(e * blocks + b, 8, stride=0)
-                south = jnp.where(lane < 16, up[b - 1] if b else zero, up[b])
-                north = jnp.where(lane >= 112, down[b + 1] if b < blocks - 1 else zero, down[b])
-                first = (n * blocks + b) * tracers
-                fresh = diag[e, :, at] * row[b]
-                fresh = fresh + twice(east_c[spread, :]) * src[e + 1, :, at]
-                fresh = fresh + twice(west_c[spread, :]) * src[e - 1, :, at]
-                fresh = fresh + twice(lat_c[spread, :]) * (south + north)
-                fresh = fresh + vert[e, :, at] * dep[first : first + tracers]
-                fresh = fresh + force[s, e, :, at]
-                fresh = fresh + mixed[b // 2][:, b % 2 * 128 : b % 2 * 128 + 128]
-                dst[e, :, at] = jnp.where(active, fresh, row[b])
+            first = n * blocks * tracers
+            results.append(
+                (row, [dep[first + b * tracers : first + (b + 1) * tracers] for b in range(blocks)], mixed)
+            )
+        return results
+
+    def combine(src, dst, e, result, active):
+        row, dep, mixed = result
+        up = [pltpu.roll(c, 16, 1) for c in row]
+        down = [pltpu.roll(c, 112, 1) for c in row]
+        for b in range(blocks):
+            at = pl.ds(b * 128, 128)
+            spread = pl.ds(e * blocks + b, 8, stride=0)
+            south = jnp.where(lane < 16, up[b - 1] if b else zero, up[b])
+            north = jnp.where(lane >= 112, down[b + 1] if b < blocks - 1 else zero, down[b])
+            fresh = diag[e, :, at] * row[b]
+            fresh = fresh + twice(east_c[spread, :]) * src[e + 1, :, at]
+            fresh = fresh + twice(west_c[spread, :]) * src[e - 1, :, at]
+            fresh = fresh + twice(lat_c[spread, :]) * (south + north)
+            fresh = fresh + vert[e, :, at] * dep[b]
+            fresh = fresh + mixed[b // 2][:, b % 2 * 128 : b % 2 * 128 + 128]
+            dst[e, :, at] = fresh if active is None else jnp.where(active, fresh, row[b])
+
+    def update(s, level, es):
+        src, dst = fields[s][level], fields[s][level + 1]
+        active = alive(s, level) if level >= LEAST_STEPS else None
+        waiting = None
+        for i in range(0, len(es), UNROLL):
+            group = es[i : i + UNROLL]
+            results = mix(src, s, group)
+            if waiting is not None:
+                for e, result in zip(*waiting):
+                    combine(src, dst, e, result, active)
+            waiting = (group, results)
+        for e, result in zip(*waiting):
+            combine(src, dst, e, result, active)
+
+    def span(s, level, first, count):
+        def body(g, _):
+            update(s, level, [first + g * (count // 2) + n for n in range(count // 2)])
+            return 0
+
+        lax.fori_loop(0, 2, body, 0)
 
     def alive(s, level):
         return jnp.full((tracers, 128), counts[own if s == 0 else prev], jnp.int32) > level
 
     def interior(s, base):
-        def level_body(k, _):
-            active = alive(s, base + k)
-            groups = (rows - 2 - 2 * k + UNROLL - 1) // UNROLL
-            reach = rows - 2 - 2 * k - UNROLL
-
-            def body(g, _):
-                first = W + 1 + k + g * reach // (groups - 1)
-                update(s, base + k, [first + n for n in range(UNROLL)], active)
-                return 0
-
-            lax.fori_loop(0, groups, body, 0)
-            return 0
-
-        lax.fori_loop(0, HALF, level_body, 0)
+        for k in range(HALF):
+            span(s, base + k, W + 1 + k, rows - 2 - 2 * k)
 
     def edges(s, base):
-        def level_body(k, _):
-            left = W - 2 + k
-            right = W + rows - 1 - k
-            es = [left + n for n in range(3)] + [right + n for n in range(3)]
-            update(s, base + k, es, alive(s, base + k))
-            return 0
-
-        lax.fori_loop(0, HALF, level_body, 0)
+        for k in range(HALF):
+            left, right = W - 2 + k, W + rows - 1 - k
+            update(s, base + k, [left + n for n in range(3)] + [right + n for n in range(3)])
+
+    def whole(s, base):
+        for k in range(HALF):
+            span(s, base + k, 1 + k, rows + 4 - 2 * k)
 
     def residual(s, body_value):
         def body(r, acc):
             for b in range(blocks):
                 at = pl.ds(b * 128, 128)
-                value = fields[s, STEPS, r + W, :, at] - body_value(r, b)
-                fields[s, STEPS, r + W, :, at] = value
+                value = fields[s][STEPS][r + W, :, at] - body_value(r, b)
+                fields[s][STEPS][r + W, :, at] = value
                 acc = acc + value * value
             return acc
 
@@ -355,7 +386,7 @@
             sends.append(copy)
         return sends
 
-    def finish(s, sends, slot):
+    def finish(s, sends):
         for copy in sends:
             copy.wait()
         square = red[s, 0]
@@ -367,14 +398,18 @@
 
     def scale(s, root, slot):
         inverse = 1.0 / root
-        target = out.at[slot].reshape(tracers * stride, 128)
+        buffer = native.at[0] if s == 0 else near
+        target = buffer.reshape(tracers * stride, 128)
 
         def body(r, _):
             for b in range(blocks):
-                target[native_row(r, b), :] = fields[s, STEPS, r + W, :, pl.ds(b * 128, 128)] * inverse
+                target[native_row(r, b), :] = fields[s][STEPS][r + W, :, pl.ds(b * 128, 128)] * inverse
             return 0
 
         lax.fori_loop(0, rows, body, 0)
+        copy = pltpu.make_async_copy(buffer.at[:, pl.ds(0, native_rows)], out.at[slot], store_sem.at[s])
+        copy.start()
+        return copy
 
     coefficients(W + 1, rows - 2)
     forces(W + 1, rows - 2)
@@ -393,7 +428,7 @@
     for copy in halos[0][1]:
         copy.start()
 
-    g0 = fields.at[1, 0]
+    g0 = fields[1][0]
     moves[0].wait()
     unpack(near2d, g0, 0, 8)
     halos[1][0][1].start()
@@ -411,20 +446,19 @@
     for copy in moves[2:]:
         copy.wait()
     unpack(near2d, g0, 8, rows - 16)
-    interior(1, 0)
     for copy in halos[1][0]:
         copy.wait()
-    edges(1, 0)
+    whole(1, 0)
     for copy in halos[1][1]:
         copy.start()
     interior(1, HALF)
     for copy in halos[1][1]:
         copy.wait()
     edges(1, HALF)
-    sends_prev = publish(1, residual(1, lambda r, b: fields[0, 0, r + W, :, pl.ds(b * 128, 128)]))
-    mean_own, root_own = finish(0, sends_own, 1)
-    scale(0, root_own, 1)
-    mean_prev, root_prev = finish(1, sends_prev, 0)
+    sends_prev = publish(1, residual(1, lambda r, b: fields[0][0][r + W, :, pl.ds(b * 128, 128)]))
+    mean_own, root_own = finish(0, sends_own)
+    stored = [scale(0, root_own, 1)]
+    mean_prev, root_prev = finish(1, sends_prev)
 
     local = mean_own + mean_prev
     local = jnp.sum(local, axis=0, keepdims=True)
@@ -435,13 +469,15 @@
         copy = remote(year.at[seg], year.at[seg], y_send.at[p], y_recv.at[p], (peer, lon))
         copy.start()
         sends.append(copy)
-    scale(1, root_prev, 0)
+    stored.append(scale(1, root_prev, 0))
     for copy in sends:
         copy.wait()
-    whole = year[0]
+    total = year[0]
     for p in range(1, nseg):
-        whole = whole + year[p]
-    mismatch[0, 0] = jnp.sqrt(whole / (2 * nseg * tracers))[0, 0]
+        total = total + year[p]
+    for copy in stored:
+        copy.wait()
+    mismatch[0, 0] = jnp.sqrt(total / (2 * nseg * tracers))[0, 0]
 
 
 def shards(mesh, states, step_counts, land, east_flow, vert_mix, coupling, amplitude, pattern):
@@ -468,28 +504,28 @@
             jax.ShapeDtypeStruct((1, 1), F32),
         ),
         in_specs=[any_spec] * 4 + [smem] * 3 + [vmem],
-        out_specs=(vmem, smem),
+        out_specs=(any_spec, smem),
         scratch_shapes=[
-            pltpu.VMEM((2, STEPS + 1, ext, tracers, cols), F32),
-            pltpu.VMEM((2, ext, tracers, cols), F32),
-            pltpu.VMEM((ext, tracers, cols), F32),
-            pltpu.VMEM((ext, tracers, cols), F32),
-            pltpu.VMEM((ext, tracers, cols), F32),
+            *[pltpu.VMEM((ext, tracers, cols), F32)] * 10,
+            *[pltpu.VMEM((ext, tracers, cols), F32)] * 3,
+            pltpu.VMEM((ext, 2 * tracers, cols), BF16),
             pltpu.VMEM((ext * blocks, 128), F32),
             pltpu.VMEM((ext * blocks, 128), F32),
             pltpu.VMEM((ext * blocks, 128), F32),
             pltpu.VMEM((ext * blocks, 128), F32),
             pltpu.VMEM((ext * blocks, 128), F32),
-            pltpu.VMEM((tracers, stride, 128), F32),
-            pltpu.VMEM((2, tracers, stride, 128), F32),
-            pltpu.VMEM((tracers, stride, 128), F32),
+            pltpu.VMEM((tracers, stride + 8, 128), F32),
+            pltpu.VMEM((2, tracers, stride + 8, 128), F32),
+            pltpu.VMEM((tracers, stride + 8, 128), F32),
             pltpu.VMEM((stride, 128), jnp.int32),
             pltpu.VMEM((stride, 128), F32),
             pltpu.VMEM((256, 128), BF16),
             pltpu.VMEM((2, nlon, tracers, 128), F32),
             pltpu.VMEM((nseg, 8, 128), F32),
             pltpu.VMEM((2, 8, 128), F32),
+            pltpu.VMEM((tracers, 128), F32),
             dma((5,)),
+            dma((2,)),
             dma((rows // 8,)),
             dma((rows // 8,)),
             dma((2, 2, 2)),
@@ -502,7 +538,7 @@
             dma((nseg,)),
         ],
         compiler_params=pltpu.CompilerParams(
-            collective_id=0, has_side_effects=True, vmem_limit_bytes=60 * 1024 * 1024
+            collective_id=0, has_side_effects=True, vmem_limit_bytes=44 * 1024 * 1024
         ),
     )(
         tiles(states),
@@ -511,8 +547,8 @@
         tiles(east_flow),
         step_counts,
         vert_mix,
-        amplitude,
-        jnp.concatenate([coupling] * 3, axis=1),
+        amplitude.T,
+        coupling,
     )
     out = out.reshape(per, tracers, rows // 8, blocks, 8, 128)
     out = jnp.swapaxes(out, -2, -3).reshape(states.shape)

time: 73.5 us -> 72.2 us (0.982)
  local copies, waits for them, and re-layouts: 5.34 us -> 9.44 us
  Pallas kernels: 64 us -> 60 us
  other arithmetic: 1.47 us -> 0 us
    unnamed x2 -> x17, local copies, waits for them, and re-layouts: 5.34 us -> 9.44 us
    pallas_call x1, Pallas kernels: 64 us -> 60 us  [shards(): pl.pallas_call(functools.partial(kernel, dims), out_shape=(jax.ShapeDtype...]
    concatenate x1 -> x0, other arithmetic: 1.47 us -> none  [shards(): jnp.concatenate([coupling] * 3, axis=1)]
where the time goes in v1:
time: 72.2 us; the launch traced here: 71.9 us
  Pallas kernels  60 us (83%)
  local copies, waits for them, and re-layouts  9.44 us (13%)
  between operations  2.47 us (3%)
    pallas_call x1, Pallas kernels, shards(): pl.pallas_call(functools.partial(kernel, dims), out_shape=(jax.ShapeDtype...  60 us
    unnamed x17, local copies, waits for them, and re-layouts  9.44 us

profile of v1, /device:TPU:1, one launch (start us, length us, event | category | flops | bytes accessed | tf_op | source)
XLA Modules:
  0.0 71.9 jit_solution(2035683745362207054)
XLA Ops:
  0.6 0.0 copy-start
  0.6 1.9 %copy-done = f32[2,16,24,1024]{3,2,1,0:T(8,128)S(1)} copy-done((f32[2,16,24,1024]{3,2,1,0:T(8,128)S(1)}, f32[2,16,24,1024]{3,2,1,0:T(8,128)}, u32[]{:S(2)}) %copy-start) | copy-done | bytes 3145752
  2.5 0.0 copy-start.1
  2.5 1.4 %copy-done.1 = f32[16,24,1024]{2,1,0:T(8,128)S(1)} copy-done((f32[16,24,1024]{2,1,0:T(8,128)S(1)}, f32[16,24,1024]{2,1,0:T(8,128)}, u32[]{:S(2)}) %copy-start.1) | copy-done | bytes 1572888
  3.9 0.0 copy-start.2
  3.9 0.9 %copy-done.2 = s32[24,1024]{1,0:T(8,128)S(1)} copy-done((s32[24,1024]{1,0:T(8,128)S(1)}, s32[24,1024]{1,0:T(8,128)}, u32[]{:S(2)}) %copy-start.2) | copy-done | bytes 98328
  4.8 0.0 copy-start.3
  4.8 0.9 %copy-done.3 = f32[24,1024]{1,0:T(8,128)S(1)} copy-done((f32[24,1024]{1,0:T(8,128)S(1)}, f32[24,1024]{1,0:T(8,128)}, u32[]{:S(2)}) %copy-start.3) | copy-done | bytes 98328
  5.7 0.0 copy-start.4
  5.7 0.7 copy-done.4
  6.4 0.0 copy-start.5
  6.4 0.7 copy-done.5
  7.1 0.0 copy-start.6
  7.1 0.7 copy-done.6
  7.8 0.0 copy-start.7
  7.8 0.7 copy-done.7
  8.4 60.0 %shard_map.95 = (f32[2,16,192,128]{3,2,1,0:T(8,128)S(1)}, f32[1,1]{1,0:T(1,128)}) custom-call(f32[2,16,192,128]{3,2,1,0:T(8,128)S(1)} %bitcast.28, f32[16,192,128]{2,1,0:T(8,128)S(1)} %bitcast.29, s32[192,128]{1,0:T(8,128)S(1)} %bitcast.30, f32[192,128]{1,0:T(8,128)S(1)} %bitcast.31, s32[32]{0:T(128)S(1)} %copy-done.6, f32[16]{0:T(128)S(1)} %copy-done.7, ...), custom_call_target="tpu_custom_call" | custom-call | tf_op jit(solution)/shard_map/pallas_call | solution.py:500
  68.4 1.7 %copy.12 = f32[2,16,24,1024]{3,2,1,0:T(8,128)} copy(f32[2,16,24,1024]{3,2,1,0:T(8,128)S(1)} %bitcast.27) | data formatting | bytes 6291456
Async XLA Ops:
  0.6 1.9 %copy-start = (f32[2,16,24,1024]{3,2,1,0:T(8,128)S(1)}, f32[2,16,24,1024]{3,2,1,0:T(8,128)}, u32[]{:S(2)}) copy-start(f32[2,16,24,1024]{3,2,1,0:T(8,128)} %param.8) | copy-start | bytes 9437188
  2.5 1.4 %copy-start.1 = (f32[16,24,1024]{2,1,0:T(8,128)S(1)}, f32[16,24,1024]{2,1,0:T(8,128)}, u32[]{:S(2)}) copy-start(f32[16,24,1024]{2,1,0:T(8,128)} %param.15) | copy-start | bytes 4718596
  3.9 0.9 %copy-start.2 = (s32[24,1024]{1,0:T(8,128)S(1)}, s32[24,1024]{1,0:T(8,128)}, u32[]{:S(2)}) copy-start(s32[24,1024]{1,0:T(8,128)} %param.10) | copy-start | bytes 294916
  4.8 0.9 %copy-start.3 = (f32[24,1024]{1,0:T(8,128)S(1)}, f32[24,1024]{1,0:T(8,128)}, u32[]{:S(2)}) copy-start(f32[24,1024]{1,0:T(8,128)} %param.11) | copy-start | bytes 294916
  5.7 0.7 copy-start.4
  6.4 0.7 copy-start.5
  7.1 0.7 copy-start.6
  7.8 0.7 copy-start.7

commit v2 on v1

--- a/solution.py
+++ b/solution.py
@@ -136,6 +136,7 @@
     c_low = pltpu.roll(c_low, tracers, 1)
     place = lane // tracers
     on_diagonal = lane % tracers == lax.broadcasted_iota(jnp.int32, (tracers, 128), 0)
+    first_diagonal = on_diagonal & (place == 0)
     mixers = []
     for s in (own, prev):
         a_high, a_low = (
@@ -221,22 +222,21 @@
                 dst[r + W, :, pl.ds(b * 128, 128)] = value if scale is None else value * scale
             return 0
 
-        lax.fori_loop(0, count, body, 0)
+        lax.fori_loop(0, count, body, 0, unroll=2)
 
     loads[2].wait()
     f0 = fields[0][0]
-    unpack(own2d, f0, 0, W)
-    unpack(own2d, f0, rows - W, W)
-    unpack(own2d, f0, W, rows - 2 * W)
+    unpack(own2d, f0, 0, rows)
+    pl.semaphore_wait(barrier, nlon + nseg - 2)
+    for copy in moves + static + halos[0][0]:
+        copy.start()
     loads[3].wait()
     unpack(pat2d, press, 0, rows, STEP_SIZE)
-    pl.semaphore_wait(barrier, nlon + nseg - 2)
-    for copy in static + halos[0][0] + forcing + moves:
-        copy.start()
-
-    def coefficients(first, count):
-        def body(n, _):
-            e = first + n
+    for copy in forcing:
+        copy.start()
+
+    def coefficients(first, count, group):
+        def one(e, slot):
             at = lambda ref, k: ref[pl.ds((e + k) * blocks, blocks), :]
             w, w_e, w_w = at(wx, 0), at(wx, 1), at(wx, -1)
             u, u_w = at(ux, 0), at(ux, -1)
@@ -260,17 +260,21 @@
                 + w_w * jnp.minimum(u_w, 0.0)
             )
             faces = w * (above + below)
-            tot[0] = center
-            tot[1] = faces
+            tot[2 * slot] = center
+            tot[2 * slot + 1] = faces
             for b in range(blocks):
-                a = tot[0, pl.ds(b, 8, stride=0), :]
-                f = tot[1, pl.ds(b, 8, stride=0), :]
+                a = tot[2 * slot, pl.ds(b, 8, stride=0), :]
+                f = tot[2 * slot + 1, pl.ds(b, 8, stride=0), :]
                 s = pl.ds(b * 128, 128)
                 diag[e, :, s] = twice(a) - vmix * twice(f)
                 vert[e, :, s] = vmix * row_w(e, b)
+
+        def body(n, _):
+            for slot in range(group):
+                one(first + n * group + slot, slot)
             return 0
 
-        lax.fori_loop(0, count, body, 0)
+        lax.fori_loop(0, count // group, body, 0)
 
     def forces(first, count):
         def body(n, _):
@@ -282,7 +286,7 @@
                 parts[e, tracers : 2 * tracers, at] = low
             return 0
 
-        lax.fori_loop(0, count, body, 0)
+        lax.fori_loop(0, count, body, 0, unroll=2 if count % 2 == 0 else count)
 
     def mix(src, s, es):
         cells = [[src[e, :, pl.ds(b * 128, 128)] for b in range(blocks)] for e in es]
@@ -361,9 +365,15 @@
             left, right = W - 2 + k, W + rows - 1 - k
             update(s, base + k, [left + n for n in range(3)] + [right + n for n in range(3)])
 
-    def whole(s, base):
+    def rim(s, base):
         for k in range(HALF):
-            span(s, base + k, 1 + k, rows + 4 - 2 * k)
+            left, right = W - 2 + k, W + rows + 1 - k
+            count = 7 - 2 * k
+            update(s, base + k, [left + n for n in range(count)] + [right - n for n in range(count)])
+
+    def middle(s, base):
+        for k in range(HALF):
+            span(s, base + k, W + 5 - k, rows - 10 + 2 * k)
 
     def residual(s, body_value):
         def body(r, acc):
@@ -374,10 +384,10 @@
                 acc = acc + value * value
             return acc
 
-        return lax.fori_loop(0, rows, body, zero)
+        return lax.fori_loop(0, rows, body, zero, unroll=2)
 
     def publish(s, value):
-        red[s, lon] = value
+        red[s, lon] = jnp.sum(jnp.where(first_diagonal, jnp.sum(value, axis=1, keepdims=True), 0.0), axis=0, keepdims=True)
         sends = []
         for p in range(1, nlon):
             peer = (lon + p) % nlon
@@ -392,9 +402,12 @@
         square = red[s, 0]
         for p in range(1, nlon):
             square = square + red[s, p]
-        mean = jnp.broadcast_to(jnp.sum(square, axis=1, keepdims=True), (tracers, 128)) / total_cells
+        means = square / total_cells
+        mean = jnp.broadcast_to(
+            jnp.sum(jnp.where(first_diagonal, means, 0.0), axis=1, keepdims=True), (tracers, 128)
+        )
         root = jnp.sqrt(mean + EPSILON)
-        return mean, root
+        return means, root
 
     def scale(s, root, slot):
         inverse = 1.0 / root
@@ -406,20 +419,20 @@
                 target[native_row(r, b), :] = fields[s][STEPS][r + W, :, pl.ds(b * 128, 128)] * inverse
             return 0
 
-        lax.fori_loop(0, rows, body, 0)
+        lax.fori_loop(0, rows, body, 0, unroll=2)
         copy = pltpu.make_async_copy(buffer.at[:, pl.ds(0, native_rows)], out.at[slot], store_sem.at[s])
         copy.start()
         return copy
 
-    coefficients(W + 1, rows - 2)
+    coefficients(W + 1, rows - 2, 2)
     forces(W + 1, rows - 2)
     interior(0, 0)
     for copy in static:
         copy.wait()
     for copy in forcing:
         copy.wait()
-    coefficients(1, W)
-    coefficients(W + rows - 1, W)
+    coefficients(1, W, W)
+    coefficients(W + rows - 1, W, W)
     forces(1, W)
     forces(W + rows - 1, W)
     for copy in halos[0][0]:
@@ -448,9 +461,10 @@
     unpack(near2d, g0, 8, rows - 16)
     for copy in halos[1][0]:
         copy.wait()
-    whole(1, 0)
+    rim(1, 0)
     for copy in halos[1][1]:
         copy.start()
+    middle(1, 0)
     interior(1, HALF)
     for copy in halos[1][1]:
         copy.wait()
@@ -460,9 +474,8 @@
     stored = [scale(0, root_own, 1)]
     mean_prev, root_prev = finish(1, sends_prev)
 
-    local = mean_own + mean_prev
-    local = jnp.sum(local, axis=0, keepdims=True)
-    year[seg] = jnp.broadcast_to(local, (8, 128))
+    local = jnp.where(lane[0:1] < tracers, mean_own + mean_prev, 0.0)
+    year[seg] = jnp.broadcast_to(jnp.sum(local, axis=1, keepdims=True), (1, 128))
     sends = []
     for p in range(1, nseg):
         peer = (seg + p) % nseg
@@ -520,9 +533,9 @@
             pltpu.VMEM((stride, 128), jnp.int32),
             pltpu.VMEM((stride, 128), F32),
             pltpu.VMEM((256, 128), BF16),
-            pltpu.VMEM((2, nlon, tracers, 128), F32),
-            pltpu.VMEM((nseg, 8, 128), F32),
-            pltpu.VMEM((2, 8, 128), F32),
+            pltpu.VMEM((2, nlon, 1, 128), F32),
+            pltpu.VMEM((nseg, 1, 128), F32),
+            pltpu.VMEM((2 * HALF, 8, 128), F32),
             pltpu.VMEM((tracers, 128), F32),
             dma((5,)),
             dma((2,)),
@@ -541,14 +554,19 @@
             collective_id=0, has_side_effects=True, vmem_limit_bytes=44 * 1024 * 1024
         ),
     )(
-        tiles(states),
-        tiles(pattern),
-        tiles(land),
-        tiles(east_flow),
-        step_counts,
-        vert_mix,
-        amplitude.T,
-        coupling,
+        *(
+            pltpu.with_memory_space_constraint(x, pltpu.HBM)
+            for x in (
+                tiles(states),
+                tiles(pattern),
+                tiles(land),
+                tiles(east_flow),
+                step_counts,
+                vert_mix,
+                amplitude.T,
+                coupling,
+            )
+        )
     )
     out = out.reshape(per, tracers, rows // 8, blocks, 8, 128)
     out = jnp.swapaxes(out, -2, -3).reshape(states.shape)

time: 72.2 us -> 59.7 us (0.83)
  local copies, waits for them, and re-layouts: 9.44 us -> 1.67 us
  Pallas kernels: 60 us -> 55.5 us
    unnamed x17 -> x1, local copies, waits for them, and re-layouts: 9.44 us -> 1.67 us
    pallas_call x1, Pallas kernels: 60 us -> 55.5 us  [shards(): pl.pallas_call(functools.partial(kernel, dims), out_shape=(jax.ShapeDtype...]
where the time goes in v2:
time: 59.7 us; the launch traced here: 59.5 us
  Pallas kernels  55.5 us (93%)
  between operations  2.33 us (4%)
  local copies, waits for them, and re-layouts  1.67 us (3%)
    pallas_call x1, Pallas kernels, shards(): pl.pallas_call(functools.partial(kernel, dims), out_shape=(jax.ShapeDtype...  55.5 us
    unnamed x1, local copies, waits for them, and re-layouts  1.67 us

profile of v2, /device:TPU:1, one launch (start us, length us, event | category | flops | bytes accessed | tf_op | source)
XLA Modules:
  0.0 59.5 jit_solution(6309088024373703572)
XLA Ops:
  0.6 55.5 %shard_map.95 = (f32[2,16,192,128]{3,2,1,0:T(8,128)S(1)}, f32[1,1]{1,0:T(1,128)}) custom-call(f32[2,16,192,128]{3,2,1,0:T(8,128)} %bitcast.28, f32[16,192,128]{2,1,0:T(8,128)} %bitcast.29, s32[192,128]{1,0:T(8,128)} %bitcast.30, f32[192,128]{1,0:T(8,128)} %bitcast.31, s32[32]{0:T(128)} %counts.1, f32[16]{0:T(128)} %vert_mix.1, f32[16,32]{1,0:T(8,128)} %bitcast.32, ...), custom_call_target="tpu_custom_call" | custom-call | tf_op jit(solution)/shard_map/pallas_call | solution.py:513
  56.1 1.7 %copy.12 = f32[2,16,24,1024]{3,2,1,0:T(8,128)} copy(f32[2,16,24,1024]{3,2,1,0:T(8,128)S(1)} %bitcast.27) | data formatting | bytes 6291456

commit v3 on v2

--- a/solution.py
+++ b/solution.py
@@ -119,32 +119,8 @@
         pltpu.make_async_copy(pattern, native_p.at[:, pl.ds(0, native_rows)], load_sem.at[3]),
         pltpu.make_async_copy(states.at[1], native.at[1, :, pl.ds(0, native_rows)], load_sem.at[4]),
     ]
-    for copy in loads:
-        copy.start()
-
-    i = lax.broadcasted_iota(jnp.int32, (256, 128), 0) % 128
-    j = lax.broadcasted_iota(jnp.int32, (256, 128), 1)
-    apart = (i - j) * (i - j) == 1
-    shift[...] = jnp.where(apart & (i // DEPTH == j // DEPTH), 1.0, 0.0).astype(BF16)
-    own = 2 * seg
-    prev = (own + 2 * nseg - 1) % (2 * nseg)
-    vmix = column(lambda t: vert_mix[t], tracers)
-
-    lhs[...] = jnp.zeros((tracers, 128), F32)
-    lhs[:, 0:tracers] = coupling[...] * STEP_SIZE
-    c_high, c_low = (x.astype(F32) for x in split(lhs[...]))
-    c_low = pltpu.roll(c_low, tracers, 1)
-    place = lane // tracers
-    on_diagonal = lane % tracers == lax.broadcasted_iota(jnp.int32, (tracers, 128), 0)
-    first_diagonal = on_diagonal & (place == 0)
-    mixers = []
-    for s in (own, prev):
-        a_high, a_low = (
-            jnp.where(on_diagonal, x.astype(F32), 0.0)
-            for x in split(column(lambda t, s=s: amplitude[t, s], tracers))
-        )
-        joined = jnp.where(place == 0, c_high, jnp.where(place == 1, c_low, jnp.where(place == 3, a_low, a_high)))
-        mixers.append(joined.astype(BF16)[:, : 5 * tracers])
+    for copy in loads[:4]:
+        copy.start()
 
     loads[0].wait()
     loads[1].wait()
@@ -230,6 +206,32 @@
     pl.semaphore_wait(barrier, nlon + nseg - 2)
     for copy in moves + static + halos[0][0]:
         copy.start()
+    loads[4].start()
+
+    i = lax.broadcasted_iota(jnp.int32, (256, 128), 0) % 128
+    j = lax.broadcasted_iota(jnp.int32, (256, 128), 1)
+    apart = (i - j) * (i - j) == 1
+    shift[...] = jnp.where(apart & (i // DEPTH == j // DEPTH), 1.0, 0.0).astype(BF16)
+    own = 2 * seg
+    prev = (own + 2 * nseg - 1) % (2 * nseg)
+    vmix = column(lambda t: vert_mix[t], tracers)
+
+    lhs[...] = jnp.zeros((tracers, 128), F32)
+    lhs[:, 0:tracers] = coupling[...] * STEP_SIZE
+    c_high, c_low = (x.astype(F32) for x in split(lhs[...]))
+    c_low = pltpu.roll(c_low, tracers, 1)
+    place = lane // tracers
+    on_diagonal = lane % tracers == lax.broadcasted_iota(jnp.int32, (tracers, 128), 0)
+    first_diagonal = on_diagonal & (place == 0)
+    mixers = []
+    for s in (own, prev):
+        a_high, a_low = (
+            jnp.where(on_diagonal, x.astype(F32), 0.0)
+            for x in split(column(lambda t, s=s: amplitude[t, s], tracers))
+        )
+        joined = jnp.where(place == 0, c_high, jnp.where(place == 1, c_low, jnp.where(place == 3, a_low, a_high)))
+        mixers.append(joined.astype(BF16)[:, : 5 * tracers])
+
     loads[3].wait()
     unpack(pat2d, press, 0, rows, STEP_SIZE)
     for copy in forcing:
@@ -371,9 +373,14 @@
             count = 7 - 2 * k
             update(s, base + k, [left + n for n in range(count)] + [right - n for n in range(count)])
 
+    def core(s, base):
+        span(s, base, W + 5, rows - 10)
+        span(s, base + 1, W + 6, rows - 12)
+
     def middle(s, base):
-        for k in range(HALF):
-            span(s, base + k, W + 5 - k, rows - 10 + 2 * k)
+        last = W + rows - 1
+        update(s, base + 1, [W + 4, W + 5, last - 5, last - 4])
+        span(s, base + 2, W + 3, rows - 6)
 
     def residual(s, body_value):
         def body(r, acc):
@@ -453,17 +460,18 @@
     for copy in halos[0][1]:
         copy.wait()
     edges(0, HALF)
+
+    for copy in moves[2:]:
+        copy.wait()
+    unpack(near2d, g0, 8, rows - 16)
+    core(1, 0)
+    for copy in halos[1][0]:
+        copy.wait()
+    rim(1, 0)
+    for copy in halos[1][1]:
+        copy.start()
     loads[4].wait()
     sends_own = publish(0, residual(0, lambda r, b: own2d_1[native_row(r, b), :] * row_w(r + W, b)))
-
-    for copy in moves[2:]:
-        copy.wait()
-    unpack(near2d, g0, 8, rows - 16)
-    for copy in halos[1][0]:
-        copy.wait()
-    rim(1, 0)
-    for copy in halos[1][1]:
-        copy.start()
     middle(1, 0)
     interior(1, HALF)
     for copy in halos[1][1]:

time: 59.7 us -> 58.7 us (0.983)
  Pallas kernels: 55.5 us -> 54.5 us
    pallas_call x1, Pallas kernels: 55.5 us -> 54.5 us  [shards(): pl.pallas_call(functools.partial(kernel, dims), out_shape=(jax.ShapeDtype...]
where the time goes in v3:
time: 58.7 us; the launch traced here: 58.5 us
  Pallas kernels  54.5 us (93%)
  between operations  2.33 us (4%)
  local copies, waits for them, and re-layouts  1.67 us (3%)
    pallas_call x1, Pallas kernels, shards(): pl.pallas_call(functools.partial(kernel, dims), out_shape=(jax.ShapeDtype...  54.5 us
    unnamed x1, local copies, waits for them, and re-layouts  1.67 us

profile of v3, /device:TPU:1, one launch (start us, length us, event | category | flops | bytes accessed | tf_op | source)
XLA Modules:
  0.0 58.5 jit_solution(1554848316014812217)
XLA Ops:
  0.6 54.5 %shard_map.95 = (f32[2,16,192,128]{3,2,1,0:T(8,128)S(1)}, f32[1,1]{1,0:T(1,128)}) custom-call(f32[2,16,192,128]{3,2,1,0:T(8,128)} %bitcast.28, f32[16,192,128]{2,1,0:T(8,128)} %bitcast.29, s32[192,128]{1,0:T(8,128)} %bitcast.30, f32[192,128]{1,0:T(8,128)} %bitcast.31, s32[32]{0:T(128)} %counts.1, f32[16]{0:T(128)} %vert_mix.1, f32[16,32]{1,0:T(8,128)} %bitcast.32, ...), custom_call_target="tpu_custom_call" | custom-call | tf_op jit(solution)/shard_map/pallas_call | solution.py:521
  55.2 1.7 %copy.12 = f32[2,16,24,1024]{3,2,1,0:T(8,128)} copy(f32[2,16,24,1024]{3,2,1,0:T(8,128)S(1)} %bitcast.27) | data formatting | bytes 6291456
